TPU v7x, 32 devices: a whole 2x2x4 slice. The times are simulated.
32 devices in a mesh: grp: 2 (over y), gx: 4 (over z), gy: 2 (over x), gz: 2 (over core).
Axes of the slice: x: 2, y: 2, z: 4, core: 2. Of those that a mesh axis runs over, the one named last changes fastest.
Arguments:
- alignment_token_ids: int32 [128, 128], P(('grp', 'gx'), ('gy', 'gz')), parts along dimension 0, may hold values from 0 to 22
- homolog_profile: bfloat16 [128, 128, 256], P(('grp', 'gx'), ('gy', 'gz')), parts along dimension 0, may hold values from -6 to 6
- alignment_mask: int32 [128, 128], P(('grp', 'gx'), ('gy', 'gz')), parts along dimension 0, may hold values 0 or 1
- pair_features: bfloat16 [256, 128, 128], P(('grp', 'gy', 'gz'), 'gx'), parts along dimension 0, may hold values from -4 to 6
- symbol_lookup_weights: bfloat16 [23, 256], replicated, may hold values from -6 to 6
- asking_weights: bfloat16 [256, 256], replicated, may hold values from -0.375 to 0.375
- lookup_weights: bfloat16 [256, 256], replicated, may hold values from -0.375 to 0.375
- content_weights: bfloat16 [256, 256], replicated, may hold values from -0.375 to 0.375
- sigmoid_switch_weights: bfloat16 [256, 256], replicated, may hold values from -0.375 to 0.375
- resulting_weights: bfloat16 [256, 256], replicated, may hold values from -0.75 to 0.75
- pair_bias_matrix: float32 [128, 8], replicated, may hold values from -0.9 to 48
- first_factor_weights: bfloat16 [256, 32], replicated, may hold values from -0.375 to 0.375
- second_factor_weights: bfloat16 [256, 32], replicated, may hold values from -0.375 to 0.375
- outer_mixing_weight: bfloat16 [1024, 128], replicated, may hold values from -1 to 1
- widening_weight: bfloat16 [128, 512], replicated, may hold values from -0.5 to 0.5
- narrowing_weight: bfloat16 [512, 128], replicated, may hold values from -0.375 to 0.375
Outputs:
- profile_refreshed: bfloat16 [128, 128, 256], P(('grp', 'gx'), ('gy', 'gz')), parts along dimension 0
- pair_output: bfloat16 [256, 128, 128], P(('grp', 'gy', 'gz'), 'gx'), parts along dimension 0
There are 2 independent parts, one for each index of `grp`. A program takes and returns all parts, laid end to end along the dimension named above; an argument that names none is the same for every part. Nothing has to cross between parts.
All inputs are finite; a program needn't handle non-finite values. No bound on the sum of `alignment_mask` on one device may be relied on, other than what follows from the above.
Results may differ from a plain program's by a relative error of at most 0.013.
Values may be sent and summed in bfloat16 or wider, within the bound.
No kernel may reach another device: no remote copies, remote signals or barrier semaphores. Data moves between devices by JAX's collectives and lax.ppermute only.
A program may use at most 64 MiB of HBM per device.

v0:
```python
import jax
import jax.numpy as jnp
from jax import lax
from jax.sharding import PartitionSpec as P


def standardize_lastaxis(values):
    average = jnp.mean(values, axis=-1, keepdims=True)
    centred = values - average
    return centred * lax.rsqrt(jnp.mean(centred * centred, axis=-1, keepdims=True) + 1e-05)


def attend(state, queries, key_piece, value_piece, valid_piece, bias_rows):
    sequence_total, residue_total, feature_vectors = queries.shape
    piece_len = key_piece.shape[1]
    head_count = bias_rows.shape[1]
    head_size = feature_vectors // head_count
    running_max, running_sum, weighted = state
    scores = jnp.einsum(
        "sihd,sjhd->sihj",
        queries.reshape(sequence_total, residue_total, head_count, head_size),
        key_piece.reshape(sequence_total, piece_len, head_count, head_size),
        preferred_element_type=jnp.float32,
    ) * head_size ** (-0.5)
    scores = (
        scores
        + bias_rows[None]
        + ((valid_piece.astype(jnp.float32) - 1.0) * 1000000000.0)[:, None, None, :]
    )
    new_max = jnp.max(scores, axis=-1)
    rescale = jnp.exp(running_max - new_max)
    exp_scores = jnp.exp(scores - new_max[:, :, :, None])
    new_sum = running_sum * rescale + jnp.sum(exp_scores, axis=-1)
    accumulated = jnp.einsum(
        "sihj,sjhd->sihd",
        exp_scores.astype(jnp.bfloat16),
        value_piece.reshape(sequence_total, piece_len, head_count, head_size),
        preferred_element_type=jnp.float32,
    )
    new_weighted = (
        weighted.reshape(sequence_total, residue_total, head_count, head_size)
        * rescale[:, :, :, None]
        + accumulated
    )
    return (new_max, new_sum, new_weighted.reshape(sequence_total, residue_total, feature_vectors))


def local(
    alignment_token_ids,
    homolog_profile,
    alignment_mask,
    pair_features,
    symbol_lookup_weights,
    asking_weights,
    lookup_weights,
    content_weights,
    sigmoid_switch_weights,
    resulting_weights,
    pair_bias_matrix,
    first_factor_weights,
    second_factor_weights,
    outer_mixing_weight,
    widening_weight,
    narrowing_weight,
):
    sequence_total, residue_total, feature_vectors = homolog_profile.shape
    head_count = pair_bias_matrix.shape[1]
    side_width = first_factor_weights.shape[1]
    pair_width = pair_features.shape[2]
    class_labels = jnp.arange(symbol_lookup_weights.shape[0], dtype=jnp.int32)
    indicator_encoding = (alignment_token_ids[:, :, None] == class_labels).astype(jnp.bfloat16)
    profile_arriving = homolog_profile.astype(jnp.float32) + jnp.einsum(
        "srv,vc->src", indicator_encoding, symbol_lookup_weights, preferred_element_type=jnp.float32
    )
    standardized_profile = standardize_lastaxis(profile_arriving).astype(jnp.bfloat16)
    flat_rows = standardized_profile.reshape(sequence_total * residue_total, feature_vectors)

    def project(row_block, weight, row_total):
        return (
            jnp.dot(row_block, weight, preferred_element_type=jnp.float32)
            .astype(jnp.bfloat16)
            .reshape(sequence_total, row_total, feature_vectors)
        )

    queries = project(flat_rows, asking_weights, residue_total)
    sigmoid_switch = jax.nn.sigmoid(
        jnp.dot(flat_rows, sigmoid_switch_weights, preferred_element_type=jnp.float32)
    ).reshape(sequence_total, residue_total, feature_vectors)
    validity_mask = alignment_mask.astype(jnp.bfloat16)
    pair_normed = standardize_lastaxis(pair_features.astype(jnp.float32))
    bias_local = jnp.einsum(
        "ijc,ch->ihj", pair_normed, pair_bias_matrix, precision=lax.Precision.HIGHEST
    )
    bias_rows = lax.all_gather(bias_local, "gx", axis=2, tiled=True)
    start_state = (
        jnp.full((sequence_total, residue_total, head_count), -jnp.inf, jnp.float32),
        jnp.zeros((sequence_total, residue_total, head_count), jnp.float32),
        jnp.zeros((sequence_total, residue_total, feature_vectors), jnp.float32),
    )
    keys_local = project(flat_rows, lookup_weights, residue_total)
    values_local = project(flat_rows, content_weights, residue_total)
    final_state = attend(
        start_state,
        queries,
        lax.all_gather(keys_local, ("gy", "gz"), axis=1, tiled=True),
        lax.all_gather(values_local, ("gy", "gz"), axis=1, tiled=True),
        lax.all_gather(validity_mask, ("gy", "gz"), axis=1, tiled=True),
        bias_rows,
    )
    softmax_combined = (
        final_state[2].reshape(
            sequence_total, residue_total, head_count, feature_vectors // head_count
        )
        / final_state[1][:, :, :, None]
    )
    switched_result = (
        sigmoid_switch * softmax_combined.reshape(sequence_total, residue_total, feature_vectors)
    ).astype(jnp.bfloat16)
    attention_projector = jnp.dot(
        switched_result.reshape(sequence_total * residue_total, feature_vectors),
        resulting_weights,
        preferred_element_type=jnp.float32,
    )
    profile_refreshed = (
        profile_arriving
        + attention_projector.reshape(sequence_total, residue_total, feature_vectors)
    ).astype(jnp.bfloat16)
    averaged_products = (
        standardize_lastaxis(profile_refreshed.astype(jnp.float32))
        .astype(jnp.bfloat16)
        .reshape(sequence_total * residue_total, feature_vectors)
    )
    mask_floating = alignment_mask.astype(jnp.float32)[:, :, None]
    left_side = (
        (
            jnp.dot(
                averaged_products, first_factor_weights, preferred_element_type=jnp.float32
            ).reshape(sequence_total, residue_total, side_width)
            * mask_floating
        )
        .astype(jnp.bfloat16)
        .reshape(sequence_total, residue_total * side_width)
    )
    right_side = (
        (
            jnp.dot(
                averaged_products, second_factor_weights, preferred_element_type=jnp.float32
            ).reshape(sequence_total, residue_total, side_width)
            * mask_floating
        )
        .astype(jnp.bfloat16)
        .reshape(sequence_total, residue_total * side_width)
    )
    left_all, mask_rows = (
        lax.all_gather(left_side, "gx", axis=0, tiled=True),
        lax.all_gather(validity_mask, "gx", axis=0, tiled=True),
    )
    right_wide, mask_wide = (
        lax.all_gather(right_side, ("gy", "gz"), axis=1, tiled=True),
        lax.all_gather(validity_mask, ("gy", "gz"), axis=1, tiled=True),
    )
    right_cols, mask_cols = (
        lax.all_to_all(right_wide, "gx", split_axis=1, concat_axis=0, tiled=True),
        lax.all_to_all(mask_wide, "gx", split_axis=1, concat_axis=0, tiled=True),
    )
    pair_count = jnp.einsum("si,sj->ij", mask_rows, mask_cols, preferred_element_type=jnp.float32)
    panel_rows = 16

    def outer_panel(panel_index):
        left_rows = lax.dynamic_slice_in_dim(
            left_all, panel_index * (panel_rows * side_width), panel_rows * side_width, 1
        )
        outer_block = jnp.einsum(
            "sa,sb->ab", left_rows, right_cols, preferred_element_type=jnp.float32
        ).astype(jnp.bfloat16)
        outer_block = (
            outer_block.reshape(panel_rows, side_width, residue_total, side_width)
            .transpose(0, 2, 1, 3)
            .reshape(panel_rows * residue_total, side_width * side_width)
        )
        return jnp.dot(
            outer_block, outer_mixing_weight, preferred_element_type=jnp.float32
        ).reshape(panel_rows, residue_total, pair_width)

    mixed_pair = lax.map(
        outer_panel, jnp.arange(residue_total // panel_rows, dtype=jnp.int32)
    ).reshape(residue_total, residue_total, pair_width)
    pair_mid = pair_features.astype(jnp.float32) + mixed_pair / (pair_count[:, :, None] + 1.0)
    trans_rows = (
        standardize_lastaxis(pair_mid)
        .astype(jnp.bfloat16)
        .reshape(residue_total * residue_total, pair_width)
    )
    expanded = jax.nn.relu(
        jnp.dot(trans_rows, widening_weight, preferred_element_type=jnp.float32)
    ).astype(jnp.bfloat16)
    pair_output = (
        pair_mid
        + jnp.dot(expanded, narrowing_weight, preferred_element_type=jnp.float32).reshape(
            residue_total, residue_total, pair_width
        )
    ).astype(jnp.bfloat16)
    return (profile_refreshed, pair_output)


def solution(mesh):
    in_specs = (
        P(("grp", "gx"), ("gy", "gz")),
        P(("grp", "gx"), ("gy", "gz"), None),
        P(("grp", "gx"), ("gy", "gz")),
        P(("grp", "gy", "gz"), "gx", None),
        P(),
        P(),
        P(),
        P(),
        P(),
        P(),
        P(),
        P(),
        P(),
        P(),
        P(),
        P(),
    )
    out_specs = (P(("grp", "gx"), ("gy", "gz"), None), P(("grp", "gy", "gz"), "gx", None))
    return jax.shard_map(local, mesh=mesh, in_specs=in_specs, out_specs=out_specs, check_vma=False)
```

profile of v0, /device:TPU:0, one launch (start us, length us, event | category | flops | bytes accessed | tf_op | source)
XLA Modules:
  0.0 149.4 jit_solution(12472776725563297926)
XLA Ops:
  7.2 0.0 copy-start
  7.2 0.0 all-gather.4.cloned.1.call-start
  7.3 1.5 fusion.43
  8.8 0.3 multiply_reduce_fusion.1
  9.0 0.2 multiply_convert_fusion.1
  9.3 0.9 convolution_convert_fusion.3
  10.2 0.0 all-gather.4.cloned.1.call-update
  10.2 0.6 fusion.42
  10.8 6.2 %all-gather = bf16[4,32,16]{1,2,0:T(8,128)(2,1)S(1)} all-gather(bf16[1,32,16]{1,2,0:T(8,128)(2,1)S(1)} %bitcast.123), channel_id=1, replica_groups=mesh['grp'=2,'gx'=4,'gy'=2,'gz'=2] {'gy','gz'}, dimensions={0}, use_global_device_ids=true | all-gather | bytes 5120 | tf_op jit(solution)/shard_map/all_gather | solution.py:107
  17.1 0.1 reshape.151
  17.2 0.1 all_to_all.32
  17.2 0.7 reshape.161
  17.9 5.3 %all-to-all-start.1 = ((bf16[4,2,256]{2,1,0:T(2,128)(2,1)}), bf16[4,2,256]{2,1,0:T(2,128)(2,1)S(1)}, u32[]{:S(2)}, u32[]{:S(2)}) async-start(bf16[4,2,256]{2,1,0:T(2,128)(2,1)} %reshape.161), calls=%async_computation.1 | async-start | bytes 8192 | tf_op jit(solution)/shard_map/all_to_all | solution.py:164
  23.3 0.9 convolution_convert_fusion.1
  24.2 0.0 all-gather.6.cloned.1.call-update
  24.2 0.2 convert_reduce_fusion
  24.4 0.4 fusion.25
  24.9 2.2 %convolution_bitcast_fusion.1 = f32[32,8,32]{2,1,0:T(8,128)S(1)} fusion(bf16[32,32,128]{2,1,0:T(8,128)(2,1)S(1)} %copy-done.1, f32[32,32]{1,0:T(8,128)S(1)} %add_rsqrt_fusion.1, f32[32,32]{1,0:T(8,128)S(1)} %broadcast_multiply_fusion.1, f32[128,8]{0,1:T(8,128)S(1)} %copy-done.15), kind=kOutput, calls=%fused_computation.31 | convolution fusion | flops 12976128 | bytes 307200 | tf_op jit(solution)/shard_map/ijc,ch->ihj/dot_general | solution.py:91
  27.1 0.1 copy.37
  27.2 0.2 convolution_convert_fusion.2
  27.5 16.1 %all_gather.23 = f32[32,8,128]{0,1,2:T(8,128)S(1)} all-gather(f32[32,8,32]{0,1,2:T(8,128)S(1)} %copy.37), channel_id=1, replica_groups=mesh['grp'=2,'gx'=4,'gy'=2,'gz'=2] {'gx'}, dimensions={2}, use_global_device_ids=true | all-gather | bytes 163840 | tf_op jit(solution)/shard_map/all_gather | solution.py:94
  43.6 1.4 reshape_reshape.3
  45.0 0.2 copy.38
  45.2 13.5 %all_gather.28 = bf16[64,32]{1,0:T(8,128)(2,1)S(1)} all-gather(bf16[16,32]{1,0:T(8,128)(2,1)S(1)} %get-tuple-element.50), channel_id=1, replica_groups=mesh['grp'=2,'gx'=4,'gy'=2,'gz'=2] {'gx'}, dimensions={0}, use_global_device_ids=true | all-gather | bytes 5120 | tf_op jit(solution)/shard_map/all_gather | solution.py:156
  58.7 0.1 reshape.162
  58.8 0.2 convolution_add_fusion.2
  59.0 2.3 %copy.35 = bf16[16,128,256]{1,2,0:T(8,128)(2,1)} copy(bf16[16,128,256]{2,1,0:T(8,128)(2,1)} %all-gather.4.cloned.1.call-done) | data formatting | bytes 2097152 | tf_op jit(solution)/shard_map/all_gather | solution.py:105
  61.3 2.3 %fusion.44 = (f32[16,32,8]{1,2,0:T(8,128)S(1)}, f32[16,32,8,128]{3,1,2,0:T(8,128)S(1)}) fusion(f32[16,128]{1,0:T(8,128)S(1)} %add_multiply_fusion, f32[32,8,128]{2,0,1:T(8,128)S(1)} %copy.38, bf16[16,128,8,32]{1,3,2,0:T(8,128)(2,1)} %bitcast.113, bf16[16,32,8,32]{3,2,1,0:T(8,128)(2,1)} %reshape_reshape.3), kind=kOutput, calls=%fused_computation.79 | convolution fusion | flops 35647488 | bytes 3563520 | tf_op jit(solution)/shard_map/sihd,sjhd->sihj/dot_general | solution.py:19
  63.6 1.3 fusion.6
  64.9 0.0 all-gather.6.cloned.1.call-done
  65.0 2.3 %copy.40 = bf16[16,128,256]{1,2,0:T(8,128)(2,1)} copy(bf16[16,128,256]{2,1,0:T(8,128)(2,1)} %all-gather.6.cloned.1.call-done) | data formatting | bytes 2097152 | tf_op jit(solution)/shard_map/all_gather | solution.py:106
  67.2 3.3 %fusion.4 = f32[16,32,8,32]{1,3,2,0:T(8,128)} fusion(bf16[16,128,8,32]{1,3,2,0:T(8,128)(2,1)} %bitcast.114, f32[16,32,8,128]{3,1,2,0:T(8,128)S(1)} %get-tuple-element.54, f32[16,32,8]{1,2,0:T(8,128)S(1)} %get-tuple-element.48, f32[16,32,8]{1,2,0:T(8,128)S(1)} %get-tuple-element.53, f32[16,32,8]{1,2,0:T(8,128)S(1)} %get-tuple-element.47), kind=kOutput, calls=%fused_computation.7 | convolution fusion | flops 34865152 | bytes 3719168 | tf_op jit(solution)/shard_map/sihj,sjhd->sihd/dot_general | solution.py:34
  70.6 2.0 %copy.41 = f32[16,32,8,32]{3,2,1,0:T(8,128)S(1)} copy(f32[16,32,8,32]{1,3,2,0:T(8,128)} %fusion.4) | data formatting | bytes 1048576 | tf_op jit(solution)/shard_map/div | solution.py:111
  72.6 1.4 reshape.144
  74.0 1.4 fusion.13
  75.4 0.3 convert_reduce_fusion.1
  75.7 0.3 fusion.27
  76.0 0.3 fusion.16
  76.3 0.2 reshape.146
  76.5 5.4 %all_gather.27 = bf16[16,4096]{1,0:T(8,128)(2,1)S(1)} all-gather(bf16[16,1024]{1,0:T(8,128)(2,1)S(1)} %reshape.146), channel_id=1, replica_groups=mesh['grp'=2,'gx'=4,'gy'=2,'gz'=2] {'gy','gz'}, dimensions={1}, use_global_device_ids=true | all-gather | bytes 163840 | tf_op jit(solution)/shard_map/all_gather | solution.py:159
  81.9 0.7 copy.51
  82.6 5.1 %all-to-all-start = ((bf16[16,4,1024]{2,0,1:T(8,128)(2,1)}), bf16[16,4,1024]{2,0,1:T(8,128)(2,1)S(1)}, u32[]{:S(2)}, u32[]{:S(2)}) async-start(bf16[16,4,1024]{2,0,1:T(8,128)(2,1)} %bitcast.93), calls=%async_computation | async-start | bytes 262144 | tf_op jit(solution)/shard_map/all_to_all | solution.py:163
  87.7 0.3 fusion.15
  88.0 0.2 reshape.145
  88.2 14.1 %all_gather.26 = bf16[64,1024]{1,0:T(8,128)(2,1)S(1)} all-gather(bf16[16,1024]{1,0:T(8,128)(2,1)S(1)} %reshape.145), channel_id=1, replica_groups=mesh['grp'=2,'gx'=4,'gy'=2,'gz'=2] {'gx'}, dimensions={0}, use_global_device_ids=true | all-gather | bytes 163840 | tf_op jit(solution)/shard_map/all_gather | solution.py:155
  102.3 37.2 %while.10 = (s32[]{:T(128)}, f32[2,16,32,128]{3,2,1,0:T(8,128)S(1)}, s32[2]{0:T(128)S(1)}, bf16[64,1024]{1,0:T(8,128)(2,1)S(1)}, bf16[64,1024]{1,0:T(8,128)(2,1)...) while((s32[]{:T(128)}, f32[2,16,32,128]{3,2,1,0:T(8,128)S(1)}, ...), condition=%wide.region_9.10_spmd, body=%wide.region_8.9_spmd.sunk | while | flops 201850880 | bytes 9109671 | solution.py:185
  102.4 0.6 dynamic_slice.12
  103.6 0.5 convolution_convert_fusion.5
  104.1 4.4 %reshape.165 = bf16[16,32,32,32]{3,2,1,0:T(8,128)(2,1)} reshape(bf16[512,1024]{1,0:T(8,128)(2,1)S(1)} %convolution_convert_fusion.5) | data formatting | bytes 2097152 | tf_op jit(solution)/shard_map/while/body/eval_jaxpr/reshape | solution.py:177
  108.4 5.9 %copy.54 = bf16[16,32,32,32]{3,2,1,0:T(8,128)(2,1)} copy(bf16[16,32,32,32]{3,1,2,0:T(8,128)(2,1)} %bitcast.107) | data formatting | bytes 2097152 | tf_op jit(solution)/shard_map/while/body/eval_jaxpr/transpose | solution.py:178
  114.3 6.2 %reshape.166 = bf16[16,32,1024]{2,1,0:T(8,128)(2,1)S(1)} reshape(bf16[16,32,32,32]{3,2,1,0:T(8,128)(2,1)} %copy.54) | data formatting | bytes 2097152 | tf_op jit(solution)/shard_map/reshape.62
  120.5 0.4 fusion.72
  121.0 0.6 dynamic_slice.12
  122.2 0.5 convolution_convert_fusion.5
  122.7 4.4 %reshape.165 = bf16[16,32,32,32]{3,2,1,0:T(8,128)(2,1)} reshape(bf16[512,1024]{1,0:T(8,128)(2,1)S(1)} %convolution_convert_fusion.5) | data formatting | bytes 2097152 | tf_op jit(solution)/shard_map/while/body/eval_jaxpr/reshape | solution.py:177
  127.0 5.9 %copy.54 = bf16[16,32,32,32]{3,2,1,0:T(8,128)(2,1)} copy(bf16[16,32,32,32]{3,1,2,0:T(8,128)(2,1)} %bitcast.107) | data formatting | bytes 2097152 | tf_op jit(solution)/shard_map/while/body/eval_jaxpr/transpose | solution.py:178
  133.0 6.2 %reshape.166 = bf16[16,32,1024]{2,1,0:T(8,128)(2,1)S(1)} reshape(bf16[16,32,32,32]{3,2,1,0:T(8,128)(2,1)} %copy.54) | data formatting | bytes 2097152 | tf_op jit(solution)/shard_map/reshape.62
  139.1 0.4 fusion.72
  139.6 0.2 bitcast_divide_fusion
  139.8 0.2 fusion.35
  140.1 0.4 multiply_reduce_fusion
  140.5 0.5 multiply_convert_fusion
  141.0 0.7 fusion.8
  141.6 0.9 add_convert_fusion
  (49 shorter events, 0.2 us)
Async XLA Ops:
  7.2 68.2 %copy-start = (bf16[256,256]{1,0:T(8,128)(2,1)S(1)}, bf16[256,256]{1,0:T(8,128)(2,1)}, u32[]{:S(2)}) copy-start(bf16[256,256]{1,0:T(8,128)(2,1)} %param.27) | copy-start | bytes 393220
  7.2 2.1 %copy-start.5 = (bf16[256,256]{1,0:T(8,128)(2,1)S(1)}, bf16[256,256]{1,0:T(8,128)(2,1)}, u32[]{:S(2)}) copy-start(bf16[256,256]{1,0:T(8,128)(2,1)} %param.24) | copy-start | bytes 393220
  7.2 3.0 %copy-start.8 = (s32[16,32]{1,0:T(8,128)S(1)}, s32[16,32]{1,0:T(8,128)}, u32[]{:S(2)}) copy-start(s32[16,32]{1,0:T(8,128)} %param.20) | copy-start | bytes 6148
  7.2 16.1 %copy-start.6 = (bf16[256,256]{1,0:T(8,128)(2,1)S(1)}, bf16[256,256]{1,0:T(8,128)(2,1)}, u32[]{:S(2)}) copy-start(bf16[256,256]{1,0:T(8,128)(2,1)} %param.25) | copy-start | bytes 393220
  7.2 17.0 %copy-start.1 = (bf16[32,32,128]{2,1,0:T(8,128)(2,1)S(1)}, bf16[32,32,128]{2,1,0:T(8,128)(2,1)}, u32[]{:S(2)}) copy-start(bf16[32,32,128]{2,1,0:T(8,128)(2,1)} %param.21) | copy-start | bytes 786436
  7.2 51.8 %all-gather.4.cloned.1.call-start = ((), (), s32[]{:S(2)}) async-start(), calls=%async_computation.2 | async-start | bytes 1310720 | tf_op jit(solution)/shard_map/all_gather | solution.py:105
  8.7 16.1 %copy-start.15 = (f32[128,8]{0,1:T(8,128)S(1)}, f32[128,8]{0,1:T(8,128)}, u32[]{:S(2)}) copy-start(f32[128,8]{0,1:T(8,128)} %param.28) | copy-start | bytes 12292
  9.0 18.2 %copy-start.7 = (bf16[256,256]{1,0:T(8,128)(2,1)S(1)}, bf16[256,256]{1,0:T(8,128)(2,1)}, u32[]{:S(2)}) copy-start(bf16[256,256]{1,0:T(8,128)(2,1)} %param.23) | copy-start | bytes 393220
  17.9 40.8 %all-to-all-start.1 = ((bf16[4,2,256]{2,1,0:T(2,128)(2,1)}), bf16[4,2,256]{2,1,0:T(2,128)(2,1)S(1)}, u32[]{:S(2)}, u32[]{:S(2)}) async-start(bf16[4,2,256]{2,1,0:T(2,128)(2,1)} %reshape.161), calls=%async_computation.1 | async-start | bytes 8192 | tf_op jit(solution)/shard_map/all_to_all | solution.py:164
  23.3 41.7 %all-gather.6.cloned.1.call-start = ((), (), s32[]{:S(2)}) async-start(), calls=%async_computation.3 | async-start | bytes 1310720 | tf_op jit(solution)/shard_map/all_gather | solution.py:106
  72.6 1.4 copy-start.10
  74.0 2.0 %copy-start.9 = (f32[16,32]{1,0:T(8,128)S(1)}, f32[16,32]{1,0:T(8,128)}, u32[]{:S(2)}) copy-start(f32[16,32]{1,0:T(8,128)} %get-tuple-element.49) | copy-start | bytes 6148
  74.0 2.0 %copy-start.13 = (bf16[256,32]{0,1:T(8,128)(2,1)S(1)}, bf16[256,32]{0,1:T(8,128)(2,1)}, u32[]{:S(2)}) copy-start(bf16[256,32]{0,1:T(8,128)(2,1)} %param.30) | copy-start | bytes 49156
  75.3 12.4 %copy-start.14 = (bf16[256,32]{0,1:T(8,128)(2,1)S(1)}, bf16[256,32]{0,1:T(8,128)(2,1)}, u32[]{:S(2)}) copy-start(bf16[256,32]{0,1:T(8,128)(2,1)} %param.29) | copy-start | bytes 49156
  75.3 27.0 %copy-start.2 = (bf16[1024,128]{1,0:T(8,128)(2,1)S(1)}, bf16[1024,128]{1,0:T(8,128)(2,1)}, u32[]{:S(2)}) copy-start(bf16[1024,128]{1,0:T(8,128)(2,1)} %param.31) | copy-start | bytes 786436
  75.4 27.0 %copy-start.3 = (f32[2,16,32,128]{3,2,1,0:T(8,128)S(1)}, f32[2,16,32,128]{3,2,1,0:T(8,128)}, u32[]{:S(2)}) copy-start(f32[2,16,32,128]{3,2,1,0:T(8,128)} %custom-call) | copy-start | bytes 1572868
  75.7 26.6 %copy-start.4 = (bf16[16,32,256]{2,1,0:T(8,128)(2,1)}, bf16[16,32,256]{2,1,0:T(8,128)(2,1)S(1)}, u32[]{:S(2)}) copy-start(bf16[16,32,256]{2,1,0:T(8,128)(2,1)S(1)} %get-tuple-element.56) | copy-start | bytes 786436
  82.6 19.7 %all-to-all-start = ((bf16[16,4,1024]{2,0,1:T(8,128)(2,1)}), bf16[16,4,1024]{2,0,1:T(8,128)(2,1)S(1)}, u32[]{:S(2)}, u32[]{:S(2)}) async-start(bf16[16,4,1024]{2,0,1:T(8,128)(2,1)} %bitcast.93), calls=%async_computation | async-start | bytes 262144 | tf_op jit(solution)/shard_map/all_to_all | solution.py:163
  139.6 1.3 copy-start.11
  139.6 1.3 copy-start.12
Sparse Core Ops, SparseCore 0:
  10.3 19.4 all-gather.3
  31.9 16.7 all-gather.5
where the time goes:
time: 150 us; the launch traced here: 149 us
  blocking collectives  55.4 us (37%)
  local copies, waits for them, and re-layouts  45.8 us (31%)
  matrix products  16.4 us (11%)
  between operations  14.5 us (10%)
  starting transfers between devices  10.4 us (7%)
  other arithmetic  5.47 us (4%)
    all_gather x1, blocking collectives, local(): bias_rows = lax.all_gather(bias_local, 'gx', axis=2, tiled=True)  16.1 us
    all_gather x1, blocking collectives, local(): lax.all_gather(left_side, 'gx', axis=0, tiled=True)  14.1 us
    all_gather x1, blocking collectives, local(): lax.all_gather(validity_mask, 'gx', axis=0, tiled=True)  13.5 us
    another operation x2, local copies, waits for them, and re-layouts  12.3 us
    transpose x2, local copies, waits for them, and re-layouts, outer_panel(): outer_block = outer_block.reshape(panel_rows, side_width, residue_total,...  11.8 us
    reshape x2, local copies, waits for them, and re-layouts, outer_panel(): outer_block.reshape(panel_rows, side_width, residue_total, side_width)  8.7 us
    all_gather x1, blocking collectives, local(): lax.all_gather(validity_mask, ('gy', 'gz'), axis=1, tiled=True)  6.22 us
    all_gather x1, blocking collectives, local(): lax.all_gather(right_side, ('gy', 'gz'), axis=1, tiled=True)  5.42 us
  transfers between devices with their start and end apart: 4, of which 0 were waited for; matrix products, arithmetic and copies ran while one was open for 9% of the time, Pallas kernels for 0%

commit v1 on v0

--- a/solution.py
+++ b/solution.py
@@ -91,7 +91,17 @@
     bias_local = jnp.einsum(
         "ijc,ch->ihj", pair_normed, pair_bias_matrix, precision=lax.Precision.HIGHEST
     )
-    bias_rows = lax.all_gather(bias_local, "gx", axis=2, tiled=True)
+    n_peers_all = lax.axis_size("gx")
+    ledger = [bias_local]
+    for dd in range(n_peers_all - 1):
+        ledger.append(
+            lax.ppermute(
+                ledger[-1], "gx", [(ii, (ii + 1) % n_peers_all) for ii in range(n_peers_all)]
+            )
+        )
+    high = jnp.concatenate(ledger[::-1], 2)
+    outcome_arr = lax.axis_index("gx")
+    bias_rows = jnp.roll(high, (outcome_arr + 1) * bias_local.shape[2], 2)
     start_state = (
         jnp.full((sequence_total, residue_total, head_count), -jnp.inf, jnp.float32),
         jnp.zeros((sequence_total, residue_total, head_count), jnp.float32),

time: 150 us -> 142 us (0.947)
  blocking collectives: 55.4 us -> 38 us
  waiting for transfers between devices: 0.06 us -> 6.59 us
  starting transfers between devices: 10.4 us -> 12.5 us
    all_gather x1 -> x0, blocking collectives: 16.1 us -> none  [local(): bias_rows = lax.all_gather(bias_local, 'gx', axis=2, tiled=True)]
    ppermute x0 -> x3, waiting for transfers between devices: none -> 6.53 us  [local(): lax.ppermute(ledger[-1], 'gx', [(ii, (ii + 1) % n_peers_all) for ii in ra...]
    ppermute x0 -> x3, starting transfers between devices: none -> 5.26 us  [local(): lax.ppermute(ledger[-1], 'gx', [(ii, (ii + 1) % n_peers_all) for ii in ra...]
    all_to_all x1, starting transfers between devices: 5.09 us -> 3.33 us  [local(): lax.all_to_all(right_wide, 'gx', split_axis=1, concat_axis=0, tiled=True)]
  transfers between devices with their start and end apart: 4 -> 7, of which waited for: 0 -> 1; matrix products, arithmetic and copies ran while one was open for 9% -> 10% of each run, Pallas kernels for 0% -> 0%
where the time goes in v1:
time: 142 us; the launch traced here: 141 us
  local copies, waits for them, and re-layouts  45.8 us (32%)
  blocking collectives  38 us (27%)
  matrix products  16.4 us (12%)
  between operations  14.5 us (10%)
  starting transfers between devices  12.5 us (9%)
  waiting for transfers between devices  6.59 us (5%)
  other arithmetic  5.57 us (4%)
    all_gather x1, blocking collectives, local(): lax.all_gather(left_side, 'gx', axis=0, tiled=True)  14.2 us
    all_gather x1, blocking collectives, local(): lax.all_gather(validity_mask, 'gx', axis=0, tiled=True)  13.2 us
    another operation x2, local copies, waits for them, and re-layouts  12.3 us
    transpose x2, local copies, waits for them, and re-layouts, outer_panel(): outer_block = outer_block.reshape(panel_rows, side_width, residue_total,...  11.8 us
    reshape x2, local copies, waits for them, and re-layouts, outer_panel(): outer_block.reshape(panel_rows, side_width, residue_total, side_width)  8.7 us
    ppermute x3, waiting for transfers between devices, local(): lax.ppermute(ledger[-1], 'gx', [(ii, (ii + 1) % n_peers_all) for ii in ra...  6.53 us
    all_gather x1, blocking collectives, local(): lax.all_gather(right_side, ('gy', 'gz'), axis=1, tiled=True)  5.42 us
    ppermute x3, starting transfers between devices, local(): lax.ppermute(ledger[-1], 'gx', [(ii, (ii + 1) % n_peers_all) for ii in ra...  5.26 us
  transfers between devices with their start and end apart: 7, of which 1 were waited for; matrix products, arithmetic and copies ran while one was open for 10% of the time, Pallas kernels for 0%

profile of v1, /device:TPU:0, one launch (start us, length us, event | category | flops | bytes accessed | tf_op | source)
XLA Modules:
  0.0 140.8 jit_solution(3309407348946778165)
XLA Ops:
  7.2 0.0 all-gather.4.cloned.1.call-start
  7.3 1.5 %fusion.49 = (f32[16,32]{1,0:T(8,128)S(1)}, f32[16,32,256]{2,1,0:T(8,128)S(1)}) fusion(bf16[23,256]{1,0:T(8,128)(2,1)} %param.22, s32[16,32]{1,0:T(8,128)} %param.18, bf16[16,32,256]{2,1,0:T(8,128)(2,1)} %param.19), kind=kOutput, calls=%fused_computation.85 | convolution fusion | flops 6433792 | bytes 802304 | tf_op jit(solution)/shard_map/srv,vc->src/dot_general | solution.py:72
  8.8 0.3 multiply_reduce_fusion.1
  9.0 0.2 multiply_convert_fusion.1
  9.3 0.9 convolution_convert_fusion.3
  10.2 0.2 convert_reduce_fusion
  10.5 0.4 fusion.30
  10.9 2.2 %convolution_bitcast_fusion.1 = f32[32,8,32]{2,1,0:T(8,128)S(1)} fusion(bf16[32,32,128]{2,1,0:T(8,128)(2,1)S(1)} %copy-done.1, f32[32,32]{1,0:T(8,128)S(1)} %add_rsqrt_fusion.1, f32[32,32]{1,0:T(8,128)S(1)} %broadcast_multiply_fusion.1, f32[128,8]{0,1:T(8,128)S(1)} %copy-done.14), kind=kOutput, calls=%fused_computation.32 | convolution fusion | flops 12976128 | bytes 307200 | tf_op jit(solution)/shard_map/ijc,ch->ihj/dot_general | solution.py:91
  13.1 3.1 %collective-permute-start = (f32[32,8,32]{2,1,0:T(8,128)S(1)}, f32[32,8,32]{2,1,0:T(8,128)S(1)}, u32[]{:S(2)}, u32[]{:S(2)}) collective-permute-start(f32[32,8,32]{2,1,0:T(8,128)S(1)} %convolution_bitcast_fusion.1), channel_id=1, source_target_pairs={{0,4},{4,8},{8,12},{12,0},{1,5},{5,9},{9,13},{13,1},{2,6},{6,10},{... | collective-permute-start | bytes 98312 | tf_op jit(solution)/shard_map/ppermute | solution.py:98
  16.2 5.2 %all-gather = bf16[4,32,16]{1,2,0:T(8,128)(2,1)S(1)} all-gather(bf16[1,32,16]{1,2,0:T(8,128)(2,1)S(1)} %bitcast.130), channel_id=1, replica_groups=mesh['grp'=2,'gx'=4,'gy'=2,'gz'=2] {'gy','gz'}, dimensions={0}, use_global_device_ids=true | all-gather | bytes 5120 | tf_op jit(solution)/shard_map/all_gather | solution.py:117
  21.4 0.1 reshape.151
  21.5 0.1 all_to_all.32
  21.5 0.7 reshape.161
  22.2 3.9 %all-to-all-start.1 = ((bf16[4,2,256]{2,1,0:T(2,128)(2,1)}), bf16[4,2,256]{2,1,0:T(2,128)(2,1)S(1)}, u32[]{:S(2)}, u32[]{:S(2)}) async-start(bf16[4,2,256]{2,1,0:T(2,128)(2,1)} %reshape.161), calls=%async_computation.1 | async-start | bytes 8192 | tf_op jit(solution)/shard_map/all_to_all | solution.py:174
  26.1 0.9 convolution_convert_fusion.1
  27.0 0.2 convolution_convert_fusion.2
  27.3 2.1 %collective-permute-start.1 = (f32[32,8,32]{2,1,0:T(8,128)S(1)}, f32[32,8,32]{2,1,0:T(8,128)S(1)}, u32[]{:S(2)}, u32[]{:S(2)}) collective-permute-start(f32[32,8,32]{2,1,0:T(8,128)S(1)} %collective-permute-done), channel_id=1, source_target_pairs={{0,4},{4,8},{8,12},{12,0},{1,5},{5,9},{9,13},{13,1},{2,6},{6,10},{... | collective-permute-start | bytes 98312 | tf_op jit(solution)/shard_map/ppermute | solution.py:98
  29.4 1.4 %reshape_reshape.3 = bf16[16,32,8,32]{3,2,1,0:T(8,128)(2,1)} reshape(bf16[512,256]{1,0:T(8,128)(2,1)S(1)} %convolution_convert_fusion.2) | data formatting | bytes 524288 | tf_op jit(solution)/shard_map/reshape;reshape | solution.py:21
  30.8 13.2 %all_gather.24 = bf16[64,32]{1,0:T(8,128)(2,1)S(1)} all-gather(bf16[16,32]{1,0:T(8,128)(2,1)S(1)} %get-tuple-element.50), channel_id=1, replica_groups=mesh['grp'=2,'gx'=4,'gy'=2,'gz'=2] {'gx'}, dimensions={0}, use_global_device_ids=true | all-gather | bytes 5120 | tf_op jit(solution)/shard_map/all_gather | solution.py:166
  44.0 0.1 reshape.162
  44.1 0.1 collective-permute-start.2
  44.2 0.2 convolution_add_fusion.2
  44.4 6.5 %collective-permute-done.2 = f32[32,8,32]{2,1,0:T(8,128)S(1)} collective-permute-done((f32[32,8,32]{2,1,0:T(8,128)S(1)}, f32[32,8,32]{2,1,0:T(8,128)S(1)}, u32[]{:S(2)}, u32[]{:S(2)}) %collective-permute-start.2) | collective-permute-done | bytes 32800 | tf_op jit(solution)/shard_map/ppermute | solution.py:98
  50.9 0.3 concatenate.6
  51.2 0.1 constant_dynamic-slice_fusion
  51.4 0.0 all-gather.4.cloned.1.call-done
  51.4 2.3 %copy.35 = bf16[16,128,256]{1,2,0:T(8,128)(2,1)} copy(bf16[16,128,256]{2,1,0:T(8,128)(2,1)} %all-gather.4.cloned.1.call-done) | data formatting | bytes 2097152 | tf_op jit(solution)/shard_map/all_gather | solution.py:115
  53.6 2.3 %fusion.9 = (f32[16,32,8]{1,2,0:T(8,128)S(1)}, f32[16,8,128,32]{2,3,1,0:T(8,128)S(1)}) fusion(f32[16,128]{1,0:T(8,128)S(1)} %add_multiply_fusion, f32[32,8,128]{2,0,1:T(8,128)S(1)} %copy.37, bf16[16,128,8,32]{1,3,2,0:T(8,128)(2,1)} %bitcast.120, bf16[16,32,8,32]{3,2,1,0:T(8,128)(2,1)} %reshape_reshape.3), kind=kOutput, calls=%fused_computation.15 | convolution fusion | flops 35647488 | bytes 3563520 | tf_op jit(solution)/shard_map/sihd,sjhd->sihj/dot_general | solution.py:19
  56.0 1.4 fusion.6
  57.3 0.7 exponential_multiply_fusion
  58.0 2.3 %copy.39 = bf16[16,128,256]{1,2,0:T(8,128)(2,1)} copy(bf16[16,128,256]{2,1,0:T(8,128)(2,1)} %all-gather.6.cloned.1.call-done) | data formatting | bytes 2097152 | tf_op jit(solution)/shard_map/all_gather | solution.py:116
  60.3 3.4 %fusion.4 = f32[16,32,8,32]{1,3,2,0:T(8,128)} fusion(bf16[16,128,8,32]{1,3,2,0:T(8,128)(2,1)} %bitcast.121, f32[16,8,128,32]{2,3,1,0:T(8,128)S(1)} %get-tuple-element.54, f32[16,32,8]{1,2,0:T(8,128)} %get-tuple-element.48, f32[16,32,8]{1,2,0:T(8,128)S(1)} %get-tuple-element.53, f32[16,32,8]{1,2,0:T(8,128)} %get-tuple-element.47, ...), kind=kOutput, calls=%fused_computation.7 | convolution fusion | flops 36438016 | bytes 3858432 | tf_op jit(solution)/shard_map/sihj,sjhd->sihd/dot_general | solution.py:34
  63.6 2.0 %copy.40 = f32[16,32,8,32]{3,2,1,0:T(8,128)S(1)} copy(f32[16,32,8,32]{1,3,2,0:T(8,128)} %fusion.4) | data formatting | bytes 1048576 | tf_op jit(solution)/shard_map/div | solution.py:121
  65.7 1.4 reshape.144
  67.1 1.4 fusion.14
  68.5 0.3 convert_reduce_fusion.1
  68.8 0.3 fusion.32
  69.1 0.3 fusion.17
  69.4 0.2 reshape.146
  69.6 5.4 %all_gather.23 = bf16[16,4096]{1,0:T(8,128)(2,1)S(1)} all-gather(bf16[16,1024]{1,0:T(8,128)(2,1)S(1)} %reshape.146), channel_id=1, replica_groups=mesh['grp'=2,'gx'=4,'gy'=2,'gz'=2] {'gy','gz'}, dimensions={1}, use_global_device_ids=true | all-gather | bytes 163840 | tf_op jit(solution)/shard_map/all_gather | solution.py:169
  75.0 0.7 copy.50
  75.7 3.3 %all-to-all-start = ((bf16[16,4,1024]{2,0,1:T(8,128)(2,1)}), bf16[16,4,1024]{2,0,1:T(8,128)(2,1)S(1)}, u32[]{:S(2)}, u32[]{:S(2)}) async-start(bf16[16,4,1024]{2,0,1:T(8,128)(2,1)} %bitcast.100), calls=%async_computation | async-start | bytes 262144 | tf_op jit(solution)/shard_map/all_to_all | solution.py:173
  79.0 0.3 fusion.16
  79.4 0.2 reshape.145
  79.5 14.2 %all_gather.22 = bf16[64,1024]{1,0:T(8,128)(2,1)S(1)} all-gather(bf16[16,1024]{1,0:T(8,128)(2,1)S(1)} %reshape.145), channel_id=1, replica_groups=mesh['grp'=2,'gx'=4,'gy'=2,'gz'=2] {'gx'}, dimensions={0}, use_global_device_ids=true | all-gather | bytes 163840 | tf_op jit(solution)/shard_map/all_gather | solution.py:165
  93.8 37.2 %while.10 = (s32[]{:T(128)}, f32[2,16,32,128]{3,2,1,0:T(8,128)S(1)}, s32[2]{0:T(128)S(1)}, bf16[64,1024]{1,0:T(8,128)(2,1)S(1)}, bf16[64,1024]{1,0:T(8,128)(2,1)...) while((s32[]{:T(128)}, f32[2,16,32,128]{3,2,1,0:T(8,128)S(1)}, ...), condition=%wide.region_9.10_spmd, body=%wide.region_8.9_spmd.sunk | while | flops 201850880 | bytes 9109671 | solution.py:195
  93.8 0.6 dynamic_slice.18
  95.1 0.5 convolution_convert_fusion.5
  95.5 4.3 %reshape.165 = bf16[16,32,32,32]{3,2,1,0:T(8,128)(2,1)} reshape(bf16[512,1024]{1,0:T(8,128)(2,1)S(1)} %convolution_convert_fusion.5) | data formatting | bytes 2097152 | tf_op jit(solution)/shard_map/while/body/eval_jaxpr/reshape | solution.py:187
  99.9 5.9 %copy.53 = bf16[16,32,32,32]{3,2,1,0:T(8,128)(2,1)} copy(bf16[16,32,32,32]{3,1,2,0:T(8,128)(2,1)} %bitcast.114) | data formatting | bytes 2097152 | tf_op jit(solution)/shard_map/while/body/eval_jaxpr/transpose | solution.py:188
  105.8 6.2 %reshape.166 = bf16[16,32,1024]{2,1,0:T(8,128)(2,1)S(1)} reshape(bf16[16,32,32,32]{3,2,1,0:T(8,128)(2,1)} %copy.53) | data formatting | bytes 2097152 | tf_op jit(solution)/shard_map/reshape.62
  111.9 0.4 fusion.77
  112.4 0.6 dynamic_slice.18
  113.7 0.5 convolution_convert_fusion.5
  114.1 4.3 %reshape.165 = bf16[16,32,32,32]{3,2,1,0:T(8,128)(2,1)} reshape(bf16[512,1024]{1,0:T(8,128)(2,1)S(1)} %convolution_convert_fusion.5) | data formatting | bytes 2097152 | tf_op jit(solution)/shard_map/while/body/eval_jaxpr/reshape | solution.py:187
  118.5 5.9 %copy.53 = bf16[16,32,32,32]{3,2,1,0:T(8,128)(2,1)} copy(bf16[16,32,32,32]{3,1,2,0:T(8,128)(2,1)} %bitcast.114) | data formatting | bytes 2097152 | tf_op jit(solution)/shard_map/while/body/eval_jaxpr/transpose | solution.py:188
  124.4 6.2 %reshape.166 = bf16[16,32,1024]{2,1,0:T(8,128)(2,1)S(1)} reshape(bf16[16,32,32,32]{3,2,1,0:T(8,128)(2,1)} %copy.53) | data formatting | bytes 2097152 | tf_op jit(solution)/shard_map/reshape.62
  130.6 0.4 fusion.77
  131.0 0.2 bitcast_divide_fusion
  131.2 0.2 fusion.40
  131.5 0.4 multiply_reduce_fusion
  131.9 0.5 multiply_convert_fusion
  132.4 0.7 fusion.8
  133.1 0.9 add_convert_fusion
  (53 shorter events, 0.2 us)
Async XLA Ops:
  7.2 61.3 %copy-start = (bf16[256,256]{1,0:T(8,128)(2,1)S(1)}, bf16[256,256]{1,0:T(8,128)(2,1)}, u32[]{:S(2)}) copy-start(bf16[256,256]{1,0:T(8,128)(2,1)} %param.27) | copy-start | bytes 393220
  7.2 2.1 %copy-start.5 = (bf16[256,256]{1,0:T(8,128)(2,1)S(1)}, bf16[256,256]{1,0:T(8,128)(2,1)}, u32[]{:S(2)}) copy-start(bf16[256,256]{1,0:T(8,128)(2,1)} %param.24) | copy-start | bytes 393220
  7.2 3.0 %copy-start.1 = (bf16[32,32,128]{2,1,0:T(8,128)(2,1)S(1)}, bf16[32,32,128]{2,1,0:T(8,128)(2,1)}, u32[]{:S(2)}) copy-start(bf16[32,32,128]{2,1,0:T(8,128)(2,1)} %param.21) | copy-start | bytes 786436
  7.2 3.7 %copy-start.14 = (f32[128,8]{0,1:T(8,128)S(1)}, f32[128,8]{0,1:T(8,128)}, u32[]{:S(2)}) copy-start(f32[128,8]{0,1:T(8,128)} %param.28) | copy-start | bytes 12292
  7.2 8.9 %copy-start.8 = (s32[16,32]{1,0:T(8,128)S(1)}, s32[16,32]{1,0:T(8,128)}, u32[]{:S(2)}) copy-start(s32[16,32]{1,0:T(8,128)} %param.20) | copy-start | bytes 6148
  7.2 18.9 %copy-start.6 = (bf16[256,256]{1,0:T(8,128)(2,1)S(1)}, bf16[256,256]{1,0:T(8,128)(2,1)}, u32[]{:S(2)}) copy-start(bf16[256,256]{1,0:T(8,128)(2,1)} %param.25) | copy-start | bytes 393220
  7.2 44.1 %all-gather.4.cloned.1.call-start = ((), (), s32[]{:S(2)}) async-start(), calls=%async_computation.2 | async-start | bytes 1310720 | tf_op jit(solution)/shard_map/all_gather | solution.py:115
  9.0 18.0 %copy-start.7 = (bf16[256,256]{1,0:T(8,128)(2,1)S(1)}, bf16[256,256]{1,0:T(8,128)(2,1)}, u32[]{:S(2)}) copy-start(bf16[256,256]{1,0:T(8,128)(2,1)} %param.23) | copy-start | bytes 393220
  13.1 14.2 %collective-permute-start = (f32[32,8,32]{2,1,0:T(8,128)S(1)}, f32[32,8,32]{2,1,0:T(8,128)S(1)}, u32[]{:S(2)}, u32[]{:S(2)}) collective-permute-start(f32[32,8,32]{2,1,0:T(8,128)S(1)} %convolution_bitcast_fusion.1), channel_id=1, source_target_pairs={{0,4},{4,8},{8,12},{12,0},{1,5},{5,9},{9,13},{13,1},{2,6},{6,10},{... | collective-permute-start | bytes 98312 | tf_op jit(solution)/shard_map/ppermute | solution.py:98
  22.2 21.8 %all-to-all-start.1 = ((bf16[4,2,256]{2,1,0:T(2,128)(2,1)}), bf16[4,2,256]{2,1,0:T(2,128)(2,1)S(1)}, u32[]{:S(2)}, u32[]{:S(2)}) async-start(bf16[4,2,256]{2,1,0:T(2,128)(2,1)} %reshape.161), calls=%async_computation.1 | async-start | bytes 8192 | tf_op jit(solution)/shard_map/all_to_all | solution.py:174
  26.1 31.9 %all-gather.6.cloned.1.call-start = ((), (), s32[]{:S(2)}) async-start(), calls=%async_computation.3 | async-start | bytes 1310720 | tf_op jit(solution)/shard_map/all_gather | solution.py:116
  27.3 16.8 %collective-permute-start.1 = (f32[32,8,32]{2,1,0:T(8,128)S(1)}, f32[32,8,32]{2,1,0:T(8,128)S(1)}, u32[]{:S(2)}, u32[]{:S(2)}) collective-permute-start(f32[32,8,32]{2,1,0:T(8,128)S(1)} %collective-permute-done), channel_id=1, source_target_pairs={{0,4},{4,8},{8,12},{12,0},{1,5},{5,9},{9,13},{13,1},{2,6},{6,10},{... | collective-permute-start | bytes 98312 | tf_op jit(solution)/shard_map/ppermute | solution.py:98
  44.1 6.8 %collective-permute-start.2 = (f32[32,8,32]{2,1,0:T(8,128)S(1)}, f32[32,8,32]{2,1,0:T(8,128)S(1)}, u32[]{:S(2)}, u32[]{:S(2)}) collective-permute-start(f32[32,8,32]{2,1,0:T(8,128)S(1)} %collective-permute-done.1), channel_id=1, source_target_pairs={{0,4},{4,8},{8,12},{12,0},{1,5},{5,9},{9,13},{13,1},{2,6},{6,10},{... | collective-permute-start | bytes 98312 | tf_op jit(solution)/shard_map/ppermute | solution.py:98
  65.6 1.4 copy-start.9
  67.1 2.0 %copy-start.12 = (bf16[256,32]{0,1:T(8,128)(2,1)S(1)}, bf16[256,32]{0,1:T(8,128)(2,1)}, u32[]{:S(2)}) copy-start(bf16[256,32]{0,1:T(8,128)(2,1)} %param.30) | copy-start | bytes 49156
  68.4 10.6 %copy-start.13 = (bf16[256,32]{0,1:T(8,128)(2,1)S(1)}, bf16[256,32]{0,1:T(8,128)(2,1)}, u32[]{:S(2)}) copy-start(bf16[256,32]{0,1:T(8,128)(2,1)} %param.29) | copy-start | bytes 49156
  68.4 25.3 %copy-start.2 = (bf16[1024,128]{1,0:T(8,128)(2,1)S(1)}, bf16[1024,128]{1,0:T(8,128)(2,1)}, u32[]{:S(2)}) copy-start(bf16[1024,128]{1,0:T(8,128)(2,1)} %param.31) | copy-start | bytes 786436
  68.4 25.3 %copy-start.3 = (f32[2,16,32,128]{3,2,1,0:T(8,128)S(1)}, f32[2,16,32,128]{3,2,1,0:T(8,128)}, u32[]{:S(2)}) copy-start(f32[2,16,32,128]{3,2,1,0:T(8,128)} %custom-call) | copy-start | bytes 1572868
  68.8 25.0 %copy-start.4 = (bf16[16,32,256]{2,1,0:T(8,128)(2,1)}, bf16[16,32,256]{2,1,0:T(8,128)(2,1)S(1)}, u32[]{:S(2)}) copy-start(bf16[16,32,256]{2,1,0:T(8,128)(2,1)S(1)} %get-tuple-element.56) | copy-start | bytes 786436
  75.7 18.1 %all-to-all-start = ((bf16[16,4,1024]{2,0,1:T(8,128)(2,1)}), bf16[16,4,1024]{2,0,1:T(8,128)(2,1)S(1)}, u32[]{:S(2)}, u32[]{:S(2)}) async-start(bf16[16,4,1024]{2,0,1:T(8,128)(2,1)} %bitcast.100), calls=%async_computation | async-start | bytes 262144 | tf_op jit(solution)/shard_map/all_to_all | solution.py:173
  131.0 1.3 copy-start.10
  131.0 1.3 copy-start.11
Sparse Core Ops, SparseCore 0:
  10.3 19.4 all-gather.3
  31.9 16.6 all-gather.5
